TPU v7x, 256 devices: a whole 4x4x8 slice. The times are simulated.
256 devices in a mesh: pts: 8 (over z_lo, core), coord: 32 (over y, z_hi, x).
Axes of the slice: x: 4, y: 4, z: 8 (z_hi: 2, z_lo: 4; z = z_hi * 4 + z_lo), core: 2. Of those that a mesh axis runs over, the one named last changes fastest.
Arguments:
- point_seed: int32 [512], P('pts'), may hold values from 0 to 16777215
- pert_seed: int32 [512, 16], P('pts'), may hold values from 0 to 16777215
- source_coef: float32 [100000], P('coord'), may hold values from -9 to 9
- w1: bfloat16 [1024, 100000], P(None, 'coord'), may hold values from -0.009765625 to 0.009765625
- b1: float32 [1024], replicated, may hold values from -3 to 3
- w2: bfloat16 [1024, 1024], replicated, may hold values from -0.1875 to 0.1875
- w3: bfloat16 [1024], replicated, may hold values from -0.1875 to 0.1875
Outputs:
- residual: float32 [512], P(('pts', 'coord'))
- grad_w1: bfloat16 [1024, 100000], P('pts', 'coord')
- grad_w2: float32 [1024, 1024], P('coord')
- grad_b1: float32 [1024], P('coord')
- grad_w3: float32 [1024], P('coord')
All inputs are finite; a program needn't handle non-finite values.
Results may differ from a plain program's by a relative error of at most 0.023.
Values may be sent and summed in bfloat16 or wider, within the bound.
A program may use at most 128 MiB of HBM per device.

v0:
```python
import math

import jax
import jax.numpy as jnp
from jax import lax
from jax.sharding import PartitionSpec as P

D = 100000


hash_factor = 73244475
NOISE_SCALE = 2.0
READOUT = 0.0625


def shuffle_bits(packed_bits):
    return packed_bits ^ lax.shift_right_logical(packed_bits, jnp.full_like(packed_bits, 16))


def mix_bits(packed_bits):
    packed_bits = shuffle_bits(packed_bits)
    packed_bits = shuffle_bits(packed_bits * hash_factor)
    return shuffle_bits(packed_bits * hash_factor)


def to_unit(packed_bits):
    return ((packed_bits & 8388607).astype(jnp.float32) + 0.5) * (1.0 / 8388608.0)


def column_keys(columns):
    return (mix_bits(columns * 4), mix_bits(columns * 4 + 1), mix_bits(columns * 4 + 2))


def perturbed_rows(point_seeds, pert_seeds, column_hash, coef_part):
    key_zero, key_one, key_two = column_hash
    count_points, count_samples = pert_seeds.shape
    uniform_point = to_unit(mix_bits(key_two[None, :] ^ point_seeds[:, None]))
    coords = 2.0 * uniform_point - 1.0
    uniform_zero = to_unit(mix_bits(key_zero[None, None, :] ^ pert_seeds[:, :, None]))
    uniform_one = to_unit(mix_bits(key_one[None, None, :] ^ pert_seeds[:, :, None]))
    noise_draw = jnp.sqrt(-2.0 * jnp.log(uniform_zero)) * jnp.cos(2.0 * jnp.pi * uniform_one)
    shifted = (coords[:, None, :] + NOISE_SCALE * noise_draw).astype(jnp.bfloat16)
    shifted = shifted.reshape(count_points * count_samples, coords.shape[1])
    squares = jnp.sum(noise_draw * noise_draw, axis=2).reshape(count_points * count_samples)
    source = jnp.sum(coef_part[None, :] * jnp.sin(jnp.pi * coords), axis=1) / math.sqrt(D)
    return (shifted, squares, source)


def hidden_pass(pre_first, squares, source, w2, w3, count_samples):
    hidden_one = jnp.tanh(pre_first).astype(jnp.bfloat16)
    pre_second = lax.dot_general(
        hidden_one, w2, (((1,), (1,)), ((), ())), preferred_element_type=jnp.float32
    )
    hidden_two = jnp.tanh(pre_second).astype(jnp.bfloat16)
    values_out = READOUT * jnp.dot(hidden_two, w3, preferred_element_type=jnp.float32)
    stein_weight = (squares - D) / (NOISE_SCALE * NOISE_SCALE * count_samples)
    per_point = (stein_weight * values_out).reshape(-1, count_samples)
    residual = jnp.sum(per_point, axis=1) - source
    grad_values = (residual[:, None] * stein_weight.reshape(-1, count_samples)).reshape(-1)
    two_float = hidden_two.astype(jnp.float32)
    grad_readout = READOUT * jnp.sum(grad_values[:, None] * two_float, axis=0)
    grad_pre_two = (
        READOUT
        * grad_values[:, None]
        * w3.astype(jnp.float32)[None, :]
        * (1.0 - two_float * two_float)
    ).astype(jnp.bfloat16)
    grad_second = lax.dot_general(
        grad_pre_two, hidden_one, (((0,), (0,)), ((), ())), preferred_element_type=jnp.float32
    )
    grad_hidden = jnp.dot(grad_pre_two, w2, preferred_element_type=jnp.float32)
    one_float = hidden_one.astype(jnp.float32)
    grad_pre_one = (grad_hidden * (1.0 - one_float * one_float)).astype(jnp.bfloat16)
    grad_bias = jnp.sum(grad_pre_one.astype(jnp.float32), axis=0)
    return (residual, grad_pre_one, grad_second, grad_bias, grad_readout, hidden_one, grad_pre_two)


def shards(point_seed, pert_seed, source_coef, w1, b1, w2, w3):
    coord_count = lax.axis_size("coord")
    coord_width = w1.shape[1]
    points_here, samples = pert_seed.shape
    rows_here = points_here * samples
    rows_local = rows_here // coord_count
    points_local = points_here // coord_count
    coord_index = lax.axis_index("coord")
    columns = coord_index * coord_width + jnp.arange(coord_width, dtype=jnp.int32)
    column_hash = column_keys(columns)
    shifted, squares, source = perturbed_rows(point_seed, pert_seed, column_hash, source_coef)
    picked = shifted
    pre_local = lax.psum_scatter(
        lax.dot_general(picked, w1, (((1,), (1,)), ((), ())), preferred_element_type=jnp.float32),
        "coord",
        scatter_dimension=0,
        tiled=True,
    )
    squares_all, source_all = lax.psum((squares, source), "coord")
    squares_local = lax.dynamic_slice_in_dim(squares_all, coord_index * rows_local, rows_local, 0)
    source_local = lax.dynamic_slice_in_dim(source_all, coord_index * points_local, points_local, 0)
    residual, grad_pre_one, grad_second, grad_bias, grad_readout, hidden_one, grad_pre_two = (
        hidden_pass(pre_local + b1[None, :], squares_local, source_local, w2, w3, samples)
    )
    grad_rows = lax.all_gather(grad_pre_one, "coord", axis=0, tiled=True)
    picked = grad_rows
    grad_first = lax.psum_scatter(
        lax.dot_general(
            picked, shifted, (((0,), (0,)), ((), ())), preferred_element_type=jnp.float32
        ).astype(jnp.bfloat16),
        "pts",
        scatter_dimension=0,
        tiled=True,
    )
    share_second, share_bias, share_readout = (
        lax.psum_scatter(
            grad_second.astype(jnp.bfloat16), "coord", scatter_dimension=0, tiled=True
        ).astype(jnp.float32),
        lax.psum_scatter(
            grad_bias.astype(jnp.bfloat16), "coord", scatter_dimension=0, tiled=True
        ).astype(jnp.float32),
        lax.psum_scatter(
            grad_readout.astype(jnp.bfloat16), "coord", scatter_dimension=0, tiled=True
        ).astype(jnp.float32),
    )
    out_second, out_bias, out_readout = (
        lax.psum(share_second.astype(jnp.bfloat16), "pts").astype(jnp.float32),
        lax.psum(share_bias.astype(jnp.bfloat16), "pts").astype(jnp.float32),
        lax.psum(share_readout.astype(jnp.bfloat16), "pts").astype(jnp.float32),
    )
    return (residual, grad_first, out_second, out_bias, out_readout)


def solution(mesh):
    return jax.shard_map(
        shards,
        mesh=mesh,
        in_specs=(P("pts"), P("pts", None), P("coord"), P(None, "coord"), P(), P(), P()),
        out_specs=(
            P(("pts", "coord")),
            P("pts", "coord"),
            P("coord", None),
            P("coord"),
            P("coord"),
        ),
        check_vma=False,
    )
```

profile of v0, /device:TPU:1, one launch (start us, length us, event | category | flops | bytes accessed | tf_op | source)
XLA Modules:
  0.0 800.5 jit_solution(16428335105259536183)
XLA Ops:
  7.2 0.0 copy-start
  7.2 0.0 reduce-scatter.6.cloned.1.call-start
  7.3 0.9 copy.17
  8.2 0.1 xor.202
  8.3 4.2 multiply_reduce_fusion
  12.4 0.0 slice-start.1
  12.5 58.9 %fusion.37 = bf16[1024,3125]{1,0:T(8,128)(2,1)S(1)} fusion(s32[3125]{0:T(1024)S(1)} %get-tuple-element.18, s32[1024]{0:T(1024)S(1)} %xor.202, s32[3125]{0:T(1024)S(1)} %shift-right-logical_xor_fusion.21, f32[64,3125]{1,0:T(8,128)S(1)} %get-tuple-element.14), kind=kLoop, calls=%fused_computation.49 | loop fusion | flops 99200000 | bytes 7229096 | tf_op jit(solution)/shard_map/convert_element_type | solution.py:42
  71.4 2.7 copy-done.5
  74.1 8.8 %fusion.67 = f32[1024,1024]{1,0:T(8,128)} fusion(bf16[1024,3125]{1,0:T(8,128)(2,1)S(1)} %fusion.37, bf16[1024,3125]{0,1:T(8,128)(2,1)S(1)} %bitcast.23), kind=kOutput, calls=%fused_computation.103 | convolution fusion | flops 6553600000 | bytes 16994304 | tf_op jit(solution)/shard_map/dot_general | solution.py:91
  83.0 0.0 reduce-scatter.6.cloned.1.call-update
  83.0 0.0 reduce-scatter.8.cloned.1.call-start
  83.1 0.0 copy-start.2
  83.1 58.9 %fusion.38 = f32[64,16]{1,0:T(8,128)S(1)} fusion(s32[3125]{0:T(1024)S(1)} %get-tuple-element.18, s32[64,16]{1,0:T(8,128)S(1)} %copy.17, s32[3125]{0:T(1024)S(1)} %shift-right-logical_xor_fusion.21), kind=kLoop, calls=%fused_computation.50 | loop fusion | flops 95998976 | bytes 33192 | tf_op jit(solution)/shard_map/reduce_sum | solution.py:44
  142.0 0.1 reshape.111
  142.0 110.4 %all-reduce.2 = (f32[1024]{0:T(1024)S(1)}, f32[64]{0:T(128)S(1)}) all-reduce(f32[1024]{0:T(1024)S(1)} %reshape.111, f32[64]{0:T(128)S(1)} %broadcast_multiply_fusion), channel_id=1, replica_groups=mesh['pts'=8,'coord'=32] {'coord'}, use_global_device_ids=true, to_apply=%region_1.0 | all-reduce | flops 1088 | bytes 8704 | tf_op jit(solution)/shard_map/psum | solution.py:96
  252.4 49.9 %reduce-scatter.6.cloned.1.call-done = f32[32,1024]{1,0:T(8,128)} async-done(((f32[1024,1024]{1,0:T(8,128)}), f32[32,1024]{1,0:T(8,128)}) %reduce-scatter.6.cloned.1.call-update) | async-done | bytes 131088 | tf_op jit(solution)/shard_map/reduce_scatter | solution.py:90
  302.4 0.9 tanh_convert_fusion
  303.3 0.7 fusion.40
  304.0 0.1 fusion.42
  304.2 0.1 reshape.112
  304.3 0.1 reduce_sum.49
  304.4 0.1 dynamic-slice_subtract_fusion
  304.5 0.1 mul.286
  304.5 0.1 mul.287
  304.6 0.1 broadcast_multiply_fusion.1
  304.7 2.1 convolution_convert_fusion.1
  306.8 0.0 reduce-scatter.8.cloned.1.call-update
  306.9 0.0 all-gather.2.cloned.1.call-start
  306.9 1.1 fusion.66
  308.1 0.0 all-gather.2.cloned.1.call-update
  308.1 0.0 all-reduce.7.cloned.1.call-start
  308.1 221.3 %reduce-scatter.8.cloned.1.call-done = bf16[32,1024]{1,0:T(8,128)(2,1)} async-done(((bf16[1024,1024]{1,0:T(8,128)(2,1)}), bf16[32,1024]{1,0:T(8,128)(2,1)}) %reduce-scatter.8.cloned.1.call-update) | async-done | bytes 65552 | tf_op jit(solution)/shard_map/reduce_scatter | solution.py:113
  529.4 0.0 all-reduce.7.cloned.1.call-update
  529.5 0.0 reduce-scatter.10.cloned.1.call-start
  529.5 108.2 %all-gather.2.cloned.1.call-done = bf16[1024,1024]{1,0:T(8,128)(2,1)} async-done(((bf16[32,1024]{1,0:T(8,128)(2,1)}), bf16[1024,1024]{1,0:T(8,128)(2,1)}) %all-gather.2.cloned.1.call-update) | async-done | bytes 2097168 | tf_op jit(solution)/shard_map/all_gather | solution.py:102
  637.7 12.0 %convolution_convert_fusion = bf16[1024,3125]{0,1:T(8,128)(2,1)} fusion(bf16[1024,1024]{1,0:T(8,128)(2,1)} %all-gather.2.cloned.1.call-done, bf16[1024,3125]{1,0:T(8,128)(2,1)} %copy-done.5), kind=kOutput, calls=%fused_computation.51 | convolution fusion | flops 6556800000 | bytes 14897152 | tf_op jit(solution)/shard_map/dot_general | solution.py:105
  649.7 9.2 %copy.19 = bf16[1024,3125]{1,0:T(8,128)(2,1)} copy(bf16[1024,3125]{0,1:T(8,128)(2,1)} %convolution_convert_fusion) | data formatting | bytes 12800000
  658.9 0.0 reduce-scatter.10.cloned.1.call-update
  658.9 0.6 dynamic-slice
  660.2 0.1 fusion.53
  660.3 96.0 %all-reduce.3 = (bf16[1024]{0:T(1024)(128)(2,1)S(1)}, bf16[1024]{0:T(1024)(128)(2,1)S(1)}) all-reduce(bf16[1024]{0:T(1024)(128)(2,1)S(1)} %get-tuple-element.15, bf16[1024]{0:T(1024)(128)(2,1)S(1)} %multiply_convert_fusion), channel_id=5, replica_groups=mesh['pts'=8,'coord'=32] {'coord'}, use_global_device_ids=true, to_apply=%region_10.0.clone | all-reduce | flops 2048 | bytes 8192
  756.2 0.1 dynamic-slice.1
  756.3 0.1 dynamic-slice.3
  756.4 32.8 %all-reduce.4 = (bf16[32]{0:T(256)(128)(2,1)S(1)}, bf16[32]{0:T(256)(128)(2,1)S(1)}) all-reduce(bf16[32]{0:T(256)(128)(2,1)S(1)} %dynamic-slice.1, bf16[32]{0:T(256)(128)(2,1)S(1)} %dynamic-slice.3), channel_id=1, replica_groups=mesh['pts'=8,'coord'=32] {'pts'}, use_global_device_ids=true, to_apply=%region_11.0 | all-reduce | flops 64 | bytes 256 | tf_op jit(solution)/shard_map/psum | solution.py:125
  789.2 0.5 convert_element_type.86
  789.7 0.5 convert_element_type.88
  790.3 1.5 convert_element_type.85
  791.8 2.2 copy.20
  (21 shorter events, 0.1 us)
Async XLA Ops:
  7.2 296.1 %copy-start = (bf16[1024,1024]{1,0:T(8,128)(2,1)S(1)}, bf16[1024,1024]{1,0:T(8,128)(2,1)}, u32[]{:S(2)}) copy-start(bf16[1024,1024]{1,0:T(8,128)(2,1)} %param.12) | copy-start | bytes 6291460
  7.2 295.2 %reduce-scatter.6.cloned.1.call-start = ((), (), s32[]{:S(2)}) async-start(), calls=%async_computation.3 | async-start | bytes 4325376 | tf_op jit(solution)/shard_map/reduce_scatter | solution.py:90
  8.3 65.8 %slice-start = ((s8[6406144]{0:T(1024)(128)(4,1)}), s8[4194304]{0:T(1024)(128)(4,1)S(1)}, s32[]{:S(2)}) async-start(s8[6406144]{0:T(1024)(128)(4,1)} %bitcast.22), calls=%async_computation.8 | async-start | bytes 8388608
  12.4 61.7 %slice-start.1 = ((s8[6406144]{0:T(1024)(128)(4,1)}), s8[2211840]{0:T(1024)(128)(4,1)S(1)}, s32[]{:S(2)}) async-start(s8[6406144]{0:T(1024)(128)(4,1)} %bitcast.22), calls=%async_computation.9 | async-start | bytes 4423680
  71.4 2.7 copy-start.5
  74.1 8.9 %copy-start.1 = (bf16[1024]{0:T(1024)(128)(2,1)S(1)}, bf16[1024]{0:T(1024)(128)(2,1)}, u32[]{:S(2)}) copy-start(bf16[1024]{0:T(1024)(128)(2,1)} %param.13) | copy-start | bytes 6148
  83.0 446.5 %reduce-scatter.8.cloned.1.call-start = ((), (), s32[]{:S(2)}) async-start(), calls=%async_computation.5 | async-start | bytes 2162688 | tf_op jit(solution)/shard_map/reduce_scatter | solution.py:113
  83.1 219.3 %copy-start.2 = (f32[1024]{0:T(1024)S(1)}, f32[1024]{0:T(1024)}, u32[]{:S(2)}) copy-start(f32[1024]{0:T(1024)} %param.11) | copy-start | bytes 12292
  304.5 345.2 %copy-start.3 = (f32[2]{0:T(128)}, f32[2]{0:T(128)S(1)}, u32[]{:S(2)}) copy-start(f32[2]{0:T(128)S(1)} %dynamic-slice_subtract_fusion) | copy-start | bytes 28
  306.9 330.8 %all-gather.2.cloned.1.call-start = ((), (), s32[]{:S(2)}) async-start(), calls=%async_computation.4 | async-start | bytes 2162688 | tf_op jit(solution)/shard_map/all_gather | solution.py:102
  308.1 482.2 %all-reduce.7.cloned.1.call-start = ((), (), s32[]{:S(2)}) async-start(), calls=%async_computation.6 | async-start | bytes 131072 | tf_op jit(solution)/shard_map/psum | solution.py:124
  529.5 262.3 %reduce-scatter.10.cloned.1.call-start = ((), (), s32[]{:S(2)}) async-start(), calls=%async_computation.7 | async-start | bytes 7372800
  649.7 9.2 %copy-start.4 = (u32[256]{0:T(256)S(1)}, u32[256]{0:T(256)}, u32[]{:S(2)}) copy-start(u32[256]{0:T(256)} %constant.76) | copy-start | bytes 3076
Sparse Core Ops, SparseCore 0:
  83.1 219.1 reduce-scatter.5
  307.0 222.4 reduce-scatter.7
  533.5 104.0 all-gather.1
  640.1 66.6 all-reduce.6
  709.2 77.9 reduce-scatter.9
where the time goes:
time: 801 us; the launch traced here: 800 us
  waiting for transfers between devices  379 us (47%)
  blocking collectives  239 us (30%)
  other arithmetic  126 us (16%)
  matrix products  25 us (3%)
  local copies, waits for them, and re-layouts  16.2 us (2%)
  between operations  14.6 us (2%)
    reduce_scatter x1, waiting for transfers between devices, shards(): lax.psum_scatter(grad_second.astype(jnp.bfloat16), 'coord', scatter_dimen...  221 us
    psum x1, blocking collectives, shards(): squares_all, source_all = lax.psum((squares, source), 'coord')  110 us
    all_gather x1, waiting for transfers between devices, shards(): grad_rows = lax.all_gather(grad_pre_one, 'coord', axis=0, tiled=True)  108 us
    unnamed x1, blocking collectives  96 us
    convert_element_type x1, other arithmetic, perturbed_rows(): (coords[:, None, :] + NOISE_SCALE * noise_draw).astype(jnp.bfloat16)  58.9 us
    reduce_sum x1, other arithmetic, perturbed_rows(): jnp.sum(noise_draw * noise_draw, axis=2)  58.9 us
    reduce_scatter x1, waiting for transfers between devices, shards(): lax.psum_scatter(lax.dot_general(picked, w1, (((1,), (1,)), ((), ())), pr...  49.9 us
    psum x1, blocking collectives, shards(): lax.psum(share_bias.astype(jnp.bfloat16), 'pts').astype(jnp.float32)  32.8 us
  transfers between devices with their start and end apart: 5, of which 3 were waited for; matrix products, arithmetic and copies ran while one was open for 11% of the time, Pallas kernels for 0%

commit v1 on v0

v1 whole, which is shorter than its diff:
```python
import math

import jax
import jax.numpy as jnp
from jax import lax
from jax.experimental import pallas as pl
from jax.experimental.pallas import tpu as pltpu
from jax.sharding import PartitionSpec as P

D = 100000
HASH = 73244475
MESH = pl.DeviceIdType.MESH
F32, BF16, I32 = jnp.float32, jnp.bfloat16, jnp.int32
SINE = (1.5707962900223675, -0.6459633598658464, 0.07968848054018324, -0.004672227923047835, 0.00015082056445751214)
LOW = 8388607
UNIT = 1.0 / 8388608.0

XY = 16
ROWS = 64
HID = 1024
WIDTH = 3125
LANES = 3200
SUB = 640
NSUB = LANES // SUB
KC = 256
WIDE = HID + 128


def shuffle_bits(v):
    return v ^ lax.shift_right_logical(v, jnp.full_like(v, 16))


def rounds(v):
    v = shuffle_bits(v * HASH)
    return shuffle_bits(v * HASH)


def sine(y, scale):
    t = y * y
    acc = t * (SINE[4] * scale) + (SINE[3] * scale)
    for c in (SINE[2], SINE[1], SINE[0]):
        acc = acc * t + (c * scale)
    return acc * y


def kernel(
    seed_ref, pseed_ref, coef_ref, w1_ref, w1t_ref, b1_ref, w2_ref, w3_ref,
    res_ref, grad_ref, g2_ref,
    w1s, w2s, zs, xs, hs, sqs, srcs, acc,
    psend, precv, ssend, srecv, zsend, zrecv, tsend, trecv,
    h1s, h2s, d2s, dbuf, dall, dt, own, bsend, brecv, tmp, lsend, lrecv, rsend, rrecv,
    gbuf, grecv, gtot, hsend, hrecv, csend, crecv, fsend, frecv,
    load_sem, p_ss, p_rs, s_ss, s_rs, z_ss, z_rs, a_ss, a_rs, b_ss, b_rs,
    l_ss, l_rs, r_ss, r_rs, g_ss, g_rs, h_ss, h_rs, c_ss, c_rs,
):
    pts, coord = lax.axis_index("pts"), lax.axis_index("coord")
    zlo, core = pts // 2, pts % 2
    mx, zh, my = coord % 4, (coord // 4) % 2, coord // 8
    me = my * 4 + mx

    def plane(t):
        return (pts, (t // 4) * 8 + zh * 4 + t % 4)

    zpeer = (pts, coord + 4 - 8 * zh)
    sibling = (pts + 1 - 2 * core, coord)

    def chip(z):
        return (z * 2 + core, coord)

    def remote(src, dst, ss, rs, device):
        return pltpu.make_async_remote_copy(src, dst, ss, rs, device_id=device, device_id_type=MESH)

    def each(lo, hi, body):
        def run(i, c):
            body(i)
            return c

        lax.fori_loop(lo, hi, run, 0)

    loads = [
        pltpu.make_async_copy(w1_ref.at[pl.ds(0, 3072)], w1s.at[pl.ds(0, 3072)], load_sem.at[0]),
        pltpu.make_async_copy(w1t_ref, w1s.at[pl.ds(3072, 128)], load_sem.at[1]),
        pltpu.make_async_copy(w2_ref, w2s, load_sem.at[2]),
    ]
    for c in loads:
        c.start()
    barrier = pltpu.get_barrier_semaphore()

    def greet(device):
        pl.semaphore_signal(barrier, inc=1, device_id=device, device_id_type=MESH)

    each(1, XY, lambda p: greet(plane((me + p) % XY)))
    greet(zpeer)
    greet(sibling)
    for p in (1, 2, 3):
        greet(chip((zlo + p) % 4))

    srcs[...] = jnp.zeros_like(srcs)
    sqs[...] = jnp.zeros_like(sqs)
    lane8 = lax.broadcasted_iota(I32, (8, 128), 1)
    row8 = lax.broadcasted_iota(I32, (8, 128), 0)

    def points(k):
        at = pl.ds(pl.multiple_of(k * 128, 128), 128)
        col = (coord * WIDTH + k * 128 + lane8) * 4
        for n in range(3):
            h = rounds(shuffle_bits(col + n))
            if n < 2:
                hs[n, :, at] = shuffle_bits(h)
        h = shuffle_bits(h)
        coef = jnp.broadcast_to(coef_ref[:, at], (8, 128))
        for g in range(8):
            v = rounds(h ^ pseed_ref[8 * g:8 * g + 8, :])
            t = (v & LOW).astype(F32) + (0.5 - 4194304.0)
            x = t * (2.0 * UNIT)
            y = t * (4.0 * UNIT)
            fold = 1.0 - jnp.abs(jnp.abs(y) - 1.0)
            s = coef * sine(jnp.where(y < 0, -fold, fold), 1.0)
            for i in range(2):
                xs[g * 2 + i, 0:4, at] = x[4 * i:4 * i + 4]
                srcs[g * 2 + i, 0:4, :] += s[4 * i:4 * i + 4]

    each(0, LANES // 128, points)

    def target(s, i):
        if i == 0:
            dx, dy = 2 * (1 - s // 2), 2 * (1 - s % 2)
        elif i == 1:
            dx, dy = 1, 3 - s
        elif i == 2:
            dx, dy = 3, (s + 1) % 4
        else:
            dx, dy = 2 * (1 - s // 2), 3 - 2 * (s % 2)
        return ((my + dy) % 4) * 4 + (mx + dx) % 4

    def noise(ts, k, width, mask):
        for l in range(width // 128):
            at = pl.ds(pl.multiple_of(k * KC + l * 128, 128), 128)
            h0, h1 = hs[0, :, at], hs[1, :, at]
            h0 = jnp.concatenate([h0, h0], axis=0)
            h1 = jnp.concatenate([h1, h1], axis=0)
            for t in ts:
                for p in range(4):
                    here = pl.ds(p * 16, 16)
                    seed = seed_ref[t, here, :]
                    u0 = ((rounds(h0 ^ seed) & LOW).astype(F32) + 0.5) * UNIT
                    r = jnp.sqrt(-2.0 * jnp.log(u0))
                    a = (rounds(h1 ^ seed) & LOW).astype(F32) + (0.5 - 4194304.0)
                    y = (jnp.abs(a) - 2097152.0) * (4.0 * UNIT)
                    e = r * sine(y, 2.0)
                    x = jnp.broadcast_to(xs[t, p:p + 1, at], (16, 128))
                    z = x + e
                    q = e * e
                    if mask is not None:
                        z = jnp.where(mask, z, 0.0)
                        q = jnp.where(mask, q, 0.0)
                    zs[t, here, at] = z.astype(BF16)
                    sqs[t, here, :] += q

    def first_layer(ts, k, width):
        at = pl.ds(pl.multiple_of(k * KC, 128), width)
        left = jnp.concatenate([zs[t, :, at] for t in ts], axis=0)
        acc[...] += jnp.dot(left, w1s[at, :], preferred_element_type=F32)

    eye = jnp.where(
        lax.broadcasted_iota(I32, (ROWS, 128), 0) == lax.broadcasted_iota(I32, (ROWS, 128), 1), 1.0, 0.0
    )
    tail_mask = lax.broadcasted_iota(I32, (16, 128), 1) < WIDTH - 3072

    def stats_of(t):
        sq = jnp.sum(sqs[t], axis=1, keepdims=True)
        row_sq = jnp.sum(eye * sq, axis=0, keepdims=True)
        src = jnp.sum(srcs[t], axis=1, keepdims=True)
        row_src = jnp.sum(jnp.where(lane8 // 16 == row8, src, 0.0), axis=0, keepdims=True)
        return jnp.where(row8 == 0, row_sq, jnp.where(row8 == 1, row_src, 0.0))

    def partial_copy(t, slot):
        return remote(psend.at[t], precv.at[slot], p_ss.at[t], p_rs.at[slot], plane(t))

    def stat_copy(t, slot):
        return remote(ssend.at[t], srecv.at[slot], s_ss.at[t], s_rs.at[slot], plane(t))

    loads[0].wait()
    loads[1].wait()

    def step(s):
        ts = [target(s, i) for i in range(4)]
        acc[...] = jnp.zeros_like(acc)
        noise(ts, 0, KC, None)

        def inner(k):
            first_layer(ts, k - 1, KC)
            noise(ts, k, KC, None)

        each(1, 12, inner)
        first_layer(ts, 11, KC)
        noise(ts, 12, 128, tail_mask)
        first_layer(ts, 12, 128)

        @pl.when(s == 0)
        def _():
            pl.semaphore_wait(barrier, XY - 1 + 5)

        for i, t in enumerate(ts):
            value = acc[i * ROWS:(i + 1) * ROWS, :].astype(BF16)
            tile = stats_of(t)
            if i > 0:
                psend[t] = value
                ssend[t] = tile
                partial_copy(t, me).start()
                stat_copy(t, me).start()
                continue

            @pl.when(s < 3)
            def _():
                psend[t] = value
                ssend[t] = tile
                partial_copy(t, me).start()
                stat_copy(t, me).start()

            @pl.when(s == 3)
            def _():
                precv[me] = value
                srecv[me] = tile

    each(0, 4, step)

    def arrived(p):
        slot = (me + p) % XY
        partial_copy(slot, slot).wait_recv()
        stat_copy(slot, slot).wait_recv()

    each(1, XY, arrived)

    def plane_sum(r):
        at = pl.ds(pl.multiple_of(r * 16, 16), 16)
        tot = precv[0, at, :].astype(F32)
        for n in range(1, XY):
            tot += precv[n, at, :].astype(F32)
        zsend[at, :] = tot.astype(BF16)

    each(0, ROWS // 16, plane_sum)
    tot = srecv[0]
    for n in range(1, XY):
        tot += srecv[n]
    tsend[...] = tot
    z_copy = remote(zsend, zrecv, z_ss.at[0], z_rs.at[0], zpeer)
    t_copy = remote(tsend, trecv, z_ss.at[1], z_rs.at[1], zpeer)
    z_copy.start()
    t_copy.start()
    loads[2].wait()
    z_copy.wait_recv()
    t_copy.wait_recv()

    pre = (zsend[...].astype(F32) + zrecv[...].astype(F32)) + b1_ref[...]
    h1 = jnp.tanh(pre).astype(BF16)
    h1s[...] = h1
    two = jnp.tanh(
        lax.dot_general(h1, w2s[...], (((1,), (1,)), ((), ())), preferred_element_type=F32)
    ).astype(BF16)
    stat = tsend[...] + trecv[...]
    sq = jnp.sum(eye * stat[0:1, :], axis=1, keepdims=True) * 0.25
    src = jnp.sum(eye * stat[1:2, :], axis=1, keepdims=True) / math.sqrt(D)
    two_float = two.astype(F32)
    w3 = w3_ref[...]
    value = 0.0625 * jnp.sum(two_float * w3, axis=1, keepdims=True)
    stein = (sq - D) / 64.0
    prod = jnp.broadcast_to(stein * value, (ROWS, 128)).reshape(4, 16, 128)
    residual = jnp.broadcast_to(jnp.sum(prod, axis=1, keepdims=True), (4, 16, 128)).reshape(ROWS, 128) - src
    res_ref[...] = jnp.zeros_like(res_ref)
    for n in range(2):
        @pl.when(zh == n)
        def _():
            res_ref[0:1, :] = residual[32 * n:32 * n + 1, :]
            res_ref[1:2, :] = residual[32 * n + 16:32 * n + 17, :]

    dval = residual * stein
    dpre2 = (0.0625 * dval[:, 0:1] * w3 * (1.0 - two_float * two_float)).astype(BF16)
    back = jnp.dot(dpre2, w2s[...], preferred_element_type=F32)
    one_float = h1.astype(F32)
    dpre1 = (back * (1.0 - one_float * one_float)).astype(BF16)
    for j in range(4):
        part = dpre1[:, 256 * j:256 * j + 256]
        dbuf[j] = part
        dall[j, me] = part
        h2s[j] = two[:, 256 * j:256 * j + 256]
        d2s[j] = dpre2[:, 256 * j:256 * j + 256]

    def gather_copy(j, t, slot):
        return remote(dbuf.at[j], dall.at[j, slot], a_ss.at[j * XY + t], a_rs.at[j * XY + slot], plane(t))

    for j in (3, 0, 2, 1):
        each(1, XY, lambda p, j=j: gather_copy(j, (me + p) % XY, me).start())

    lane64 = lax.broadcasted_iota(I32, (ROWS, 128), 1)
    high = dval.astype(BF16)
    low = (dval - high.astype(F32)).astype(BF16)
    zero = jnp.zeros_like(dval)
    pick0 = jnp.where(lane64 == 0, 1.0, zero).astype(BF16)
    pick1 = jnp.where(lane64 == 1, high.astype(F32), jnp.where(lane64 == 2, low.astype(F32), zero)).astype(BF16)
    rows_of = (((0,), (0,)), ((), ()))
    half = pl.ds(pl.multiple_of(zh * 128, 128), 128)
    for j in range(4):
        main = lax.dot_general(d2s[j, :, half], h1, rows_of, preferred_element_type=F32)
        more = lax.dot_general(dbuf[j, :, half], pick0, rows_of, preferred_element_type=F32)
        more += lax.dot_general(h2s[j, :, half], pick1, rows_of, preferred_element_type=F32)
        gbuf[j, :, 0:HID] = main.astype(BF16)
        gbuf[j, :, HID:WIDE] = more.astype(BF16)
    grecv[me] = gbuf[my, pl.ds(pl.multiple_of(mx * 32, 32), 32), :]

    def small_copy(t, slot):
        mine = gbuf.at[t // 4, pl.ds(pl.multiple_of((t % 4) * 32, 32), 32)]
        return remote(mine, grecv.at[slot], g_ss.at[t], g_rs.at[slot], plane(t))

    each(1, XY, lambda p: small_copy((me + p) % XY, me).start())

    def core_copy(n):
        return remote(bsend.at[n], brecv.at[n], b_ss.at[n], b_rs.at[n], sibling)

    def chunk(j):
        def there(p):
            slot = (me + p) % XY
            gather_copy(j, slot, slot).wait_recv()

        each(1, XY, there)
        for n, c in enumerate((1 - core, core)):
            block = dall[j, :, :, pl.ds(pl.multiple_of(c * 128, 128), 128)].reshape(XY * ROWS, 128)
            dt[128 * n:128 * n + 128, :] = jnp.transpose(block)

        def sub(b):
            at = pl.ds(pl.multiple_of(b * SUB, 128), SUB)
            right = zs[:, :, at].reshape(XY * ROWS, SUB)
            part = jnp.dot(dt[...], right, preferred_element_type=F32)
            n = j * NSUB + b
            bsend[n] = part[0:128].astype(BF16)
            core_copy(n).start()
            own[n] = part[128:256]

        each(0, NSUB, sub)

    def right_copy(n):
        return remote(lsend.at[n], lrecv.at[n], l_ss.at[n], l_rs.at[n], chip(zlo + 1))

    def left_copy(n):
        return remote(rsend.at[n], rrecv.at[n], r_ss.at[n], r_rs.at[n], chip(zlo - 1))

    def chip_sum(n):
        core_copy(n).wait_recv()
        return own[n] + brecv[n].astype(F32)

    def go_right(t, b):
        n = t * NSUB + b
        tmp[...] = chip_sum((3 - t) * NSUB + b)

        @pl.when(zlo > 0)
        def _():
            remote(lsend.at[n], lrecv.at[n], l_ss.at[n], l_rs.at[n], chip(zlo - 1)).wait_recv()
            tmp[...] += lrecv[n].astype(F32)

        lsend[n] = tmp[...].astype(BF16)
        right_copy(n).start()

    def go_left(t, b):
        n = t * NSUB + b
        tmp[...] = chip_sum(n)

        @pl.when(zlo < 3)
        def _():
            remote(rsend.at[n], rrecv.at[n], r_ss.at[n], r_rs.at[n], chip(zlo + 1)).wait_recv()
            tmp[...] += rrecv[n].astype(F32)

        rsend[n] = tmp[...].astype(BF16)
        left_copy(n).start()

    each(0, 2, lambda q: chunk(3 - 3 * q))

    @pl.when(zlo == 0)
    def _():
        each(0, NSUB, lambda b: go_right(0, b))

    @pl.when(zlo == 3)
    def _():
        each(0, NSUB, lambda b: go_left(0, b))

    each(0, 2, lambda q: chunk(2 - q))

    def small_there(p):
        slot = (me + p) % XY
        small_copy(slot, slot).wait_recv()

    each(1, XY, small_there)
    for r in range(2):
        at = slice(16 * r, 16 * r + 16)
        tot = grecv[0, at, :].astype(F32)
        for n in range(1, XY):
            tot += grecv[n, at, :].astype(F32)
        gtot[at, :] = tot
    theirs = pl.ds(pl.multiple_of(16 * (1 - core), 16), 16)
    mine = pl.ds(pl.multiple_of(16 * core, 16), 16)
    hsend[...] = gtot[theirs, :].astype(BF16)
    h_copy = remote(hsend, hrecv, h_ss.at[0], h_rs.at[0], sibling)
    h_copy.start()

    def line(t):
        def both(b):
            @pl.when((3 - t > zlo) & (zlo > (0 if t == 0 else -1)))
            def _():
                go_right(t, b)

            @pl.when((t < zlo) & (zlo < (3 if t == 0 else 4)))
            def _():
                go_left(t, b)

        each(0, NSUB, both)

    def across(z, slot):
        return remote(csend, crecv.at[slot], c_ss.at[z], c_rs.at[slot], chip(z))

    line(0)
    h_copy.wait_recv()
    total = (gtot[mine, :] + hrecv[...].astype(F32)).astype(BF16)
    csend[...] = total
    crecv[zlo] = total
    for p in (1, 2, 3):
        across((zlo + p) % 4, zlo).start()
    line(1)
    for p in (1, 2, 3):
        across((zlo + p) % 4, (zlo + p) % 4).wait_recv()
    total = crecv[0].astype(F32)
    for n in range(1, 4):
        total += crecv[n].astype(F32)
    fsend[...] = total
    g2_ref[mine, :] = total
    f_copy = remote(fsend, frecv, h_ss.at[1], h_rs.at[1], sibling)
    f_copy.start()
    line(2)
    f_copy.wait_recv()
    g2_ref[theirs, :] = frecv[...]

    def finish(b):
        tmp[...] = chip_sum(zlo * NSUB + b)

        @pl.when(zlo > 0)
        def _():
            n = (3 - zlo) * NSUB + b
            remote(lsend.at[n], lrecv.at[n], l_ss.at[n], l_rs.at[n], chip(zlo - 1)).wait_recv()
            tmp[...] += lrecv[n].astype(F32)

        @pl.when(zlo < 3)
        def _():
            n = zlo * NSUB + b
            remote(rsend.at[n], rrecv.at[n], r_ss.at[n], r_rs.at[n], chip(zlo + 1)).wait_recv()
            tmp[...] += rrecv[n].astype(F32)

        grad_ref[:, pl.ds(pl.multiple_of(b * SUB, 128), SUB)] = tmp[...].astype(BF16)

    each(0, NSUB, finish)

    def left_plane(p):
        t = (me + p) % XY
        partial_copy(t, me).wait_send()
        stat_copy(t, me).wait_send()
        small_copy(t, me).wait_send()
        for j in range(4):
            gather_copy(j, t, me).wait_send()

    each(1, XY, left_plane)
    z_copy.wait_send()
    t_copy.wait_send()
    h_copy.wait_send()
    f_copy.wait_send()
    for p in (1, 2, 3):
        across((zlo + p) % 4, zlo).wait_send()
    each(0, 4 * NSUB, lambda n: core_copy(n).wait_send())
    each(0, (3 - zlo) * NSUB, lambda n: right_copy(n).wait_send())
    each(0, zlo * NSUB, lambda n: left_copy(n).wait_send())


def shards(point_seed, pert_seed, source_coef, w1, b1, w2, w3):
    seeds = shuffle_bits(pert_seed).reshape(4, 2, 4, 2, 16).transpose(0, 2, 1, 3, 4)
    seeds = jnp.broadcast_to(seeds.reshape(XY, ROWS)[:, :, None], (XY, ROWS, 128))
    pseeds = shuffle_bits(point_seed).reshape(4, 2, 4, 2).transpose(0, 2, 1, 3)
    pseeds = jnp.broadcast_to(pseeds.reshape(64)[:, None], (64, 128))
    coef = jnp.pad(source_coef, (0, LANES - WIDTH)).reshape(1, LANES)
    w1t = w1.T
    tail = jnp.pad(w1t[3072:], ((0, LANES - WIDTH), (0, 0)))
    vmem = pl.BlockSpec(memory_space=pltpu.VMEM)
    anyw = pl.BlockSpec(memory_space=pl.ANY)
    dma = lambda n: pltpu.SemaphoreType.DMA((n,))
    v = pltpu.VMEM
    n15, n20 = 3 * NSUB, 4 * NSUB
    residual, grad, small = pl.pallas_call(
        kernel,
        name="pinn_step",
        out_shape=(
            jax.ShapeDtypeStruct((8, 128), F32),
            jax.ShapeDtypeStruct((128, LANES), BF16),
            jax.ShapeDtypeStruct((32, WIDE), F32),
        ),
        in_specs=[vmem, vmem, vmem, anyw, anyw, vmem, anyw, vmem],
        out_specs=(vmem, vmem, vmem),
        scratch_shapes=[
            v((LANES, HID), BF16), v((HID, HID), BF16), v((XY, ROWS, LANES), BF16),
            v((XY, 8, LANES), F32), v((2, 8, LANES), I32), v((XY, ROWS, 128), F32), v((XY, 8, 128), F32),
            v((256, HID), F32),
            v((XY, ROWS, HID), BF16), v((XY, ROWS, HID), BF16), v((XY, 8, 128), F32), v((XY, 8, 128), F32),
            v((ROWS, HID), BF16), v((ROWS, HID), BF16), v((8, 128), F32), v((8, 128), F32),
            v((ROWS, HID), BF16), v((4, ROWS, 256), BF16), v((4, ROWS, 256), BF16), v((4, ROWS, 256), BF16),
            v((4, XY, ROWS, 256), BF16), v((256, XY * ROWS), BF16),
            v((n20, 128, SUB), F32), v((n20, 128, SUB), BF16), v((n20, 128, SUB), BF16), v((128, SUB), F32),
            v((n15, 128, SUB), BF16), v((n15, 128, SUB), BF16), v((n15, 128, SUB), BF16), v((n15, 128, SUB), BF16),
            v((4, 128, WIDE), BF16), v((XY, 32, WIDE), BF16), v((32, WIDE), F32),
            v((16, WIDE), BF16), v((16, WIDE), BF16), v((16, WIDE), BF16), v((4, 16, WIDE), BF16),
            v((16, WIDE), F32), v((16, WIDE), F32),
            dma(3), dma(XY), dma(XY), dma(XY), dma(XY), dma(2), dma(2), dma(4 * XY), dma(4 * XY), dma(n20), dma(n20),
            dma(n15), dma(n15), dma(n15), dma(n15), dma(XY), dma(XY), dma(2), dma(2), dma(4), dma(4),
        ],
        compiler_params=pltpu.CompilerParams(
            collective_id=0, has_side_effects=True, vmem_limit_bytes=66_000_000
        ),
    )(seeds, pseeds, coef, w1t, tail, b1.reshape(1, HID), w2, w3.astype(F32).reshape(1, HID))
    return (
        residual[0:2, 0],
        grad[:, :WIDTH],
        small[:, :HID],
        small[:, HID],
        0.0625 * (small[:, HID + 1] + small[:, HID + 2]),
    )


def solution(mesh):
    return jax.shard_map(
        shards,
        mesh=mesh,
        in_specs=(P("pts"), P("pts", None), P("coord"), P(None, "coord"), P(), P(), P()),
        out_specs=(
            P(("pts", "coord")),
            P("pts", "coord"),
            P("coord", None),
            P("coord"),
            P("coord"),
        ),
        check_vma=False,
    )
```

time: 801 us -> 185 us (0.23)
  the two profiles are of different devices: /device:TPU:1 before, /device:TPU:62 now
where the time goes in v1:
time: 185 us
  Pallas kernels  170 us (92%)
  local copies, waits for them, and re-layouts  10.1 us (5%)
  other arithmetic  4.21 us (2%)
    pallas_call x1, Pallas kernels, shards(): pl.pallas_call(kernel, name='pinn_step', out_shape=(jax.ShapeDtypeStruct(...  170 us

profile of v1, /device:TPU:62, one launch (start us, length us, event | category | flops | bytes accessed | tf_op | source)
XLA Modules:
  0.0 184.6 jit_solution(13035034378759963675)
XLA Ops:
  0.6 0.7 shift-right-logical_xor_fusion.1
  1.3 1.3 reshape.38
  2.6 0.7 shift-right-logical_xor_fusion
  3.3 0.1 reshape.33
  3.4 0.1 broadcast_in_dim.24
  3.5 0.7 pad.8
  4.2 0.6 reshape.34.coef_ref
  4.9 0.1 copy.24
  5.0 0.1 broadcast_in_dim.21
  5.0 0.7 broadcast_in_dim.25.pseed_ref
  5.7 0.9 slice.28
  6.6 0.7 pad.9.w1t_ref
  7.4 1.0 broadcast_in_dim.22.seed_ref
  8.4 169.6 %pinn_step.1 = (f32[8,128]{1,0:T(8,128)}, bf16[128,3200]{1,0:T(8,128)(2,1)}, f32[32,1152]{1,0:T(8,128)}) custom-call(s32[16,64,128]{2,1,0:T(8,128)} %broadcast_in_dim.22.seed_ref, s32[64,128]{1,0:T(8,128)} %broadcast_in_dim.25.pseed_ref, f32[1,3200]{1,0:T(1,128)} %reshape.34.coef_ref, bf16[3125,1024]{1,0:T(8,128)(2,1)} %bitcast.9, ...), custom_call_target="tpu_custom_call" | custom-call | tf_op jit(solution)/shard_map/pinn_step/pallas_call | solution.py:492
  177.9 1.3 slice_reduce_fusion.1
  179.2 2.2 %copy.27 = bf16[128,3125]{0,1:T(8,128)(2,1)} copy(bf16[128,3125]{1,0:T(8,128)(2,1)} %bitcast.10) | data formatting | bytes 1600000
  181.4 1.6 multiply_reduce_fusion
  183.0 1.6 slice.24
  (2 shorter events, 0.0 us)

commit v2 on v1

--- a/solution.py
+++ b/solution.py
@@ -22,8 +22,27 @@
 LANES = 3200
 SUB = 640
 NSUB = LANES // SUB
+LAG = 2
 KC = 256
 WIDE = HID + 128
+
+TREE = (
+    ((2, 2), (1, 0)), ((2, 1), (0, 1)), ((2, -1), (-1, 0)), ((-1, 2), (0, -1)),
+    ((1, 2), (0, 1)), ((2, 0), (1, 0)), ((0, 2), (0, -1)), ((-1, -1), (-1, 0)),
+    ((1, 1), (1, 0)), ((-1, 1), (0, 1)), ((1, -1), (0, -1)), ((0, -1), (0, -1)),
+    ((1, 0), (1, 0)), ((-1, 0), (-1, 0)), ((0, 1), (0, 1)), ((0, 0), None),
+)
+
+
+def lands(n):
+    (a, b), move = TREE[n]
+    if move is None:
+        return None
+    return tuple((v + 1) % 4 - 1 for v in (a - move[0], b - move[1]))
+
+
+CHILDREN = [[m for m in range(XY) if lands(m) == TREE[n][0]] for n in range(XY)]
+assert all(m // 4 < n // 4 for n in range(XY - 1) for m in CHILDREN[n])
 
 
 def shuffle_bits(v):
@@ -44,9 +63,9 @@
 
 
 def kernel(
-    seed_ref, pseed_ref, coef_ref, w1_ref, w1t_ref, b1_ref, w2_ref, w3_ref,
+    pert_ref, point_ref, coef_ref, w1_ref, w1t_ref, b1_ref, w2_ref, w3_ref,
     res_ref, grad_ref, g2_ref,
-    w1s, w2s, zs, xs, hs, sqs, srcs, acc,
+    seed_ref, pseed_ref, w1s, w2s, zs, xs, hs, sqs, srcs, acc,
     psend, precv, ssend, srecv, zsend, zrecv, tsend, trecv,
     h1s, h2s, d2s, dbuf, dall, dt, own, bsend, brecv, tmp, lsend, lrecv, rsend, rrecv,
     gbuf, grecv, gtot, hsend, hrecv, csend, crecv, fsend, frecv,
@@ -94,6 +113,16 @@
     greet(sibling)
     for p in (1, 2, 3):
         greet(chip((zlo + p) % 4))
+
+    for n in range(64):
+        pos = ((n // 16) * 4 + (n // 2) % 4, ((n // 8) % 2) * 2 + n % 2)
+        seed = jnp.broadcast_to(pert_ref[:, n:n + 1], (16, 128))
+        seed_ref[pos[0], 16 * pos[1]:16 * pos[1] + 16, :] = shuffle_bits(seed)
+    r64 = lax.broadcasted_iota(I32, (64, 64), 0)
+    place = (((r64 // 16) * 2 + (r64 // 2) % 2) * 4 + (r64 // 4) % 4) * 2 + r64 % 2
+    spread = jnp.where(place == lax.broadcasted_iota(I32, (64, 64), 1), point_ref[...].astype(F32), 0.0)
+    spread = jnp.sum(spread, axis=1, keepdims=True).astype(I32)
+    pseed_ref[...] = shuffle_bits(jnp.broadcast_to(spread, (64, 128)))
 
     srcs[...] = jnp.zeros_like(srcs)
     sqs[...] = jnp.zeros_like(sqs)
@@ -121,17 +150,6 @@
                 srcs[g * 2 + i, 0:4, :] += s[4 * i:4 * i + 4]
 
     each(0, LANES // 128, points)
-
-    def target(s, i):
-        if i == 0:
-            dx, dy = 2 * (1 - s // 2), 2 * (1 - s % 2)
-        elif i == 1:
-            dx, dy = 1, 3 - s
-        elif i == 2:
-            dx, dy = 3, (s + 1) % 4
-        else:
-            dx, dy = 2 * (1 - s // 2), 3 - 2 * (s % 2)
-        return ((my + dy) % 4) * 4 + (mx + dx) % 4
 
     def noise(ts, k, width, mask):
         for l in range(width // 128):
@@ -174,21 +192,34 @@
         row_src = jnp.sum(jnp.where(lane8 // 16 == row8, src, 0.0), axis=0, keepdims=True)
         return jnp.where(row8 == 0, row_sq, jnp.where(row8 == 1, row_src, 0.0))
 
-    def partial_copy(t, slot):
-        return remote(psend.at[t], precv.at[slot], p_ss.at[t], p_rs.at[slot], plane(t))
-
-    def stat_copy(t, slot):
-        return remote(ssend.at[t], srecv.at[slot], s_ss.at[t], s_rs.at[slot], plane(t))
+    def toward(move):
+        (dx, dy) = move
+        return (pts, ((my + dy + 4) % 4) * 8 + zh * 4 + (mx + dx + 4) % 4)
+
+    def partial_copy(n):
+        return remote(psend.at[n], precv.at[n], p_ss.at[n], p_rs.at[n], toward(TREE[n][1]))
+
+    def stat_copy(n):
+        return remote(ssend.at[n], srecv.at[n], s_ss.at[n], s_rs.at[n], toward(TREE[n][1]))
+
+    def gathered(n, i, t):
+        value, tile = acc[i * ROWS:(i + 1) * ROWS, :], stats_of(t)
+        for child in CHILDREN[n]:
+            partial_copy(child).wait_recv()
+            stat_copy(child).wait_recv()
+            value += precv[child].astype(F32)
+            tile += srecv[child]
+        return value.astype(BF16), tile
 
     loads[0].wait()
     loads[1].wait()
 
-    def step(s):
-        ts = [target(s, i) for i in range(4)]
+    for s in range(4):
+        ts = [((my + b + 4) % 4) * 4 + (mx + a + 4) % 4 for (a, b), _ in TREE[4 * s:4 * s + 4]]
         acc[...] = jnp.zeros_like(acc)
         noise(ts, 0, KC, None)
 
-        def inner(k):
+        def inner(k, ts=ts):
             first_layer(ts, k - 1, KC)
             noise(ts, k, KC, None)
 
@@ -196,54 +227,20 @@
         first_layer(ts, 11, KC)
         noise(ts, 12, 128, tail_mask)
         first_layer(ts, 12, 128)
-
-        @pl.when(s == 0)
-        def _():
+        if s == 0:
             pl.semaphore_wait(barrier, XY - 1 + 5)
-
         for i, t in enumerate(ts):
-            value = acc[i * ROWS:(i + 1) * ROWS, :].astype(BF16)
-            tile = stats_of(t)
-            if i > 0:
-                psend[t] = value
-                ssend[t] = tile
-                partial_copy(t, me).start()
-                stat_copy(t, me).start()
-                continue
-
-            @pl.when(s < 3)
-            def _():
-                psend[t] = value
-                ssend[t] = tile
-                partial_copy(t, me).start()
-                stat_copy(t, me).start()
-
-            @pl.when(s == 3)
-            def _():
-                precv[me] = value
-                srecv[me] = tile
-
-    each(0, 4, step)
-
-    def arrived(p):
-        slot = (me + p) % XY
-        partial_copy(slot, slot).wait_recv()
-        stat_copy(slot, slot).wait_recv()
-
-    each(1, XY, arrived)
-
-    def plane_sum(r):
-        at = pl.ds(pl.multiple_of(r * 16, 16), 16)
-        tot = precv[0, at, :].astype(F32)
-        for n in range(1, XY):
-            tot += precv[n, at, :].astype(F32)
-        zsend[at, :] = tot.astype(BF16)
-
-    each(0, ROWS // 16, plane_sum)
-    tot = srecv[0]
-    for n in range(1, XY):
-        tot += srecv[n]
-    tsend[...] = tot
+            n = 4 * s + i
+            value, tile = gathered(n, i, t)
+            if n < XY - 1:
+                psend[n] = value
+                ssend[n] = tile
+                partial_copy(n).start()
+                stat_copy(n).start()
+            else:
+                zsend[...] = value
+                tsend[...] = tile
+
     z_copy = remote(zsend, zrecv, z_ss.at[0], z_rs.at[0], zpeer)
     t_copy = remote(tsend, trecv, z_ss.at[1], z_rs.at[1], zpeer)
     z_copy.start()
@@ -262,17 +259,16 @@
     sq = jnp.sum(eye * stat[0:1, :], axis=1, keepdims=True) * 0.25
     src = jnp.sum(eye * stat[1:2, :], axis=1, keepdims=True) / math.sqrt(D)
     two_float = two.astype(F32)
-    w3 = w3_ref[...]
+    w3 = w3_ref[...].astype(F32)
     value = 0.0625 * jnp.sum(two_float * w3, axis=1, keepdims=True)
     stein = (sq - D) / 64.0
     prod = jnp.broadcast_to(stein * value, (ROWS, 128)).reshape(4, 16, 128)
     residual = jnp.broadcast_to(jnp.sum(prod, axis=1, keepdims=True), (4, 16, 128)).reshape(ROWS, 128) - src
-    res_ref[...] = jnp.zeros_like(res_ref)
     for n in range(2):
         @pl.when(zh == n)
         def _():
-            res_ref[0:1, :] = residual[32 * n:32 * n + 1, :]
-            res_ref[1:2, :] = residual[32 * n + 16:32 * n + 17, :]
+            first = lax.broadcasted_iota(I32, (1, 128), 1) == 0
+            res_ref[0:1, :] = jnp.where(first, residual[32 * n:32 * n + 1, :], residual[32 * n + 16:32 * n + 17, :])
 
     dval = residual * stein
     dpre2 = (0.0625 * dval[:, 0:1] * w3 * (1.0 - two_float * two_float)).astype(BF16)
@@ -289,8 +285,14 @@
     def gather_copy(j, t, slot):
         return remote(dbuf.at[j], dall.at[j, slot], a_ss.at[j * XY + t], a_rs.at[j * XY + slot], plane(t))
 
-    for j in (3, 0, 2, 1):
-        each(1, XY, lambda p, j=j: gather_copy(j, (me + p) % XY, me).start())
+    inside, upper = zlo * (3 - zlo) // 2, zlo // 2
+
+    def order(q):
+        base = (1 - inside) * (3 - q) + inside * ((q % 2) * (q // 2) + (1 - q % 2) * (3 - q // 2))
+        return upper * 3 + (1 - 2 * upper) * base
+
+    for q in range(4):
+        each(1, XY, lambda p, q=q: gather_copy(order(q), (me + p) % XY, me).start())
 
     lane64 = lax.broadcasted_iota(I32, (ROWS, 128), 1)
     high = dval.astype(BF16)
@@ -372,17 +374,27 @@
         rsend[n] = tmp[...].astype(BF16)
         left_copy(n).start()
 
-    each(0, 2, lambda q: chunk(3 - 3 * q))
-
-    @pl.when(zlo == 0)
-    def _():
-        each(0, NSUB, lambda b: go_right(0, b))
-
-    @pl.when(zlo == 3)
-    def _():
-        each(0, NSUB, lambda b: go_left(0, b))
-
-    each(0, 2, lambda q: chunk(2 - q))
+    def onward(n):
+        r, l = n - LAG * upper, n - LAG * (1 - upper)
+
+        @pl.when((r >= 0) & (r < (3 - zlo) * NSUB))
+        def _():
+            go_right(r // NSUB, r % NSUB)
+
+        @pl.when((l >= 0) & (l < zlo * NSUB))
+        def _():
+            go_left(l // NSUB, l % NSUB)
+
+    def columns(q):
+        chunk(order(q))
+        lo = (1 - inside) * q * NSUB
+        hi = (1 - inside) * (q * NSUB + NSUB) + inside * (q // 2) * (1 - q % 2) * (2 * NSUB + LAG)
+
+        @pl.when(q < 3)
+        def _():
+            each(lo, hi, onward)
+
+    each(0, 4, columns)
 
     def small_there(p):
         slot = (me + p) % XY
@@ -401,41 +413,31 @@
     h_copy = remote(hsend, hrecv, h_ss.at[0], h_rs.at[0], sibling)
     h_copy.start()
 
-    def line(t):
-        def both(b):
-            @pl.when((3 - t > zlo) & (zlo > (0 if t == 0 else -1)))
-            def _():
-                go_right(t, b)
-
-            @pl.when((t < zlo) & (zlo < (3 if t == 0 else 4)))
-            def _():
-                go_left(t, b)
-
-        each(0, NSUB, both)
-
     def across(z, slot):
         return remote(csend, crecv.at[slot], c_ss.at[z], c_rs.at[slot], chip(z))
 
-    line(0)
     h_copy.wait_recv()
     total = (gtot[mine, :] + hrecv[...].astype(F32)).astype(BF16)
     csend[...] = total
     crecv[zlo] = total
     for p in (1, 2, 3):
         across((zlo + p) % 4, zlo).start()
-    line(1)
     for p in (1, 2, 3):
         across((zlo + p) % 4, (zlo + p) % 4).wait_recv()
     total = crecv[0].astype(F32)
     for n in range(1, 4):
         total += crecv[n].astype(F32)
     fsend[...] = total
-    g2_ref[mine, :] = total
+    gtot[mine, :] = total
     f_copy = remote(fsend, frecv, h_ss.at[1], h_rs.at[1], sibling)
     f_copy.start()
-    line(2)
     f_copy.wait_recv()
-    g2_ref[theirs, :] = frecv[...]
+    gtot[theirs, :] = frecv[...]
+    g2_ref[...] = gtot[:, 0:HID]
+    small = gtot[:, HID:WIDE]
+    eye32 = eye[0:32, :]
+    res_ref[2:3, :] = jnp.sum(eye32 * small[:, 0:1], axis=0, keepdims=True)
+    res_ref[3:4, :] = 0.0625 * jnp.sum(eye32 * (small[:, 1:2] + small[:, 2:3]), axis=0, keepdims=True)
 
     def finish(b):
         tmp[...] = chip_sum(zlo * NSUB + b)
@@ -458,13 +460,14 @@
 
     def left_plane(p):
         t = (me + p) % XY
-        partial_copy(t, me).wait_send()
-        stat_copy(t, me).wait_send()
         small_copy(t, me).wait_send()
         for j in range(4):
             gather_copy(j, t, me).wait_send()
 
     each(1, XY, left_plane)
+    for n in range(XY - 1):
+        partial_copy(n).wait_send()
+        stat_copy(n).wait_send()
     z_copy.wait_send()
     t_copy.wait_send()
     h_copy.wait_send()
@@ -477,11 +480,7 @@
 
 
 def shards(point_seed, pert_seed, source_coef, w1, b1, w2, w3):
-    seeds = shuffle_bits(pert_seed).reshape(4, 2, 4, 2, 16).transpose(0, 2, 1, 3, 4)
-    seeds = jnp.broadcast_to(seeds.reshape(XY, ROWS)[:, :, None], (XY, ROWS, 128))
-    pseeds = shuffle_bits(point_seed).reshape(4, 2, 4, 2).transpose(0, 2, 1, 3)
-    pseeds = jnp.broadcast_to(pseeds.reshape(64)[:, None], (64, 128))
-    coef = jnp.pad(source_coef, (0, LANES - WIDTH)).reshape(1, LANES)
+    coef = jnp.pad(source_coef.reshape(1, WIDTH), ((0, 0), (0, LANES - WIDTH)))
     w1t = w1.T
     tail = jnp.pad(w1t[3072:], ((0, LANES - WIDTH), (0, 0)))
     vmem = pl.BlockSpec(memory_space=pltpu.VMEM)
@@ -495,12 +494,12 @@
         out_shape=(
             jax.ShapeDtypeStruct((8, 128), F32),
             jax.ShapeDtypeStruct((128, LANES), BF16),
-            jax.ShapeDtypeStruct((32, WIDE), F32),
+            jax.ShapeDtypeStruct((32, HID), F32),
         ),
         in_specs=[vmem, vmem, vmem, anyw, anyw, vmem, anyw, vmem],
         out_specs=(vmem, vmem, vmem),
         scratch_shapes=[
-            v((LANES, HID), BF16), v((HID, HID), BF16), v((XY, ROWS, LANES), BF16),
+            v((XY, ROWS, 128), I32), v((64, 128), I32), v((LANES, HID), BF16), v((HID, HID), BF16), v((XY, ROWS, LANES), BF16),
             v((XY, 8, LANES), F32), v((2, 8, LANES), I32), v((XY, ROWS, 128), F32), v((XY, 8, 128), F32),
             v((256, HID), F32),
             v((XY, ROWS, HID), BF16), v((XY, ROWS, HID), BF16), v((XY, 8, 128), F32), v((XY, 8, 128), F32),
@@ -518,14 +517,8 @@
         compiler_params=pltpu.CompilerParams(
             collective_id=0, has_side_effects=True, vmem_limit_bytes=66_000_000
         ),
-    )(seeds, pseeds, coef, w1t, tail, b1.reshape(1, HID), w2, w3.astype(F32).reshape(1, HID))
-    return (
-        residual[0:2, 0],
-        grad[:, :WIDTH],
-        small[:, :HID],
-        small[:, HID],
-        0.0625 * (small[:, HID + 1] + small[:, HID + 2]),
-    )
+    )(pert_seed.T, point_seed.reshape(1, 64), coef, w1t, tail, b1.reshape(1, HID), w2, w3.reshape(1, HID))
+    return residual[0, 0:2], grad[:, :WIDTH], small, residual[2, 0:32], residual[3, 0:32]
 
 
 def solution(mesh):

time: 185 us -> 152 us (0.82)
  the two profiles are of different devices: /device:TPU:62 before, /device:TPU:1 now
where the time goes in v2:
time: 152 us
  Pallas kernels  141 us (93%)
  local copies, waits for them, and re-layouts  10.4 us (7%)
    pallas_call x1, Pallas kernels, shards(): pl.pallas_call(kernel, name='pinn_step', out_shape=(jax.ShapeDtypeStruct(...  141 us
    unnamed x2, local copies, waits for them, and re-layouts  3.73 us

profile of v2, /device:TPU:1, one launch (start us, length us, event | category | flops | bytes accessed | tf_op | source)
XLA Modules:
  0.0 152.0 jit_solution(11298280678181139407)
XLA Ops:
  0.6 0.9 slice.20
  1.5 0.7 pad.9.w1t_ref
  2.3 0.7 reshape.23
  3.0 0.6 pad.8.coef_ref
  3.6 1.3 reshape.25.w3_ref
  4.9 140.9 %pinn_step.1 = (f32[8,128]{1,0:T(8,128)}, bf16[128,3200]{1,0:T(8,128)(2,1)}, f32[32,1024]{1,0:T(8,128)}) custom-call(s32[16,64]{1,0:T(8,128)} %bitcast.14, s32[1,64]{1,0:T(1,128)} %bitcast.16, f32[1,3200]{1,0:T(1,128)} %pad.8.coef_ref, bf16[3125,1024]{1,0:T(8,128)(2,1)} %bitcast.12, bf16[128,1024]{1,0:T(8,128)(2,1)} %pad.9.w1t_ref, f32[1,1024]{1,0:T(1,128)} %bitcast.15, ...), custom_call_target="tpu_custom_call" | custom-call | tf_op jit(solution)/shard_map/pinn_step/pallas_call | solution.py:491
  145.8 1.3 slice_bitcast_fusion
  147.0 1.2 slice_bitcast_fusion.2
  148.2 2.2 %copy.12 = bf16[128,3125]{0,1:T(8,128)(2,1)} copy(bf16[128,3125]{1,0:T(8,128)(2,1)} %bitcast.13) | data formatting | bytes 1600000
  150.4 1.6 %copy.14 = f32[32,1024]{1,0:T(8,128)} copy(f32[32,1024]{1,0:T(8,128)} %get-tuple-element.25) | data formatting | bytes 262144

commit v3 on v2

--- a/solution.py
+++ b/solution.py
@@ -125,7 +125,6 @@
     pseed_ref[...] = shuffle_bits(jnp.broadcast_to(spread, (64, 128)))
 
     srcs[...] = jnp.zeros_like(srcs)
-    sqs[...] = jnp.zeros_like(sqs)
     lane8 = lax.broadcasted_iota(I32, (8, 128), 1)
     row8 = lax.broadcasted_iota(I32, (8, 128), 0)
 
@@ -151,34 +150,40 @@
 
     each(0, LANES // 128, points)
 
-    def noise(ts, k, width, mask):
-        for l in range(width // 128):
-            at = pl.ds(pl.multiple_of(k * KC + l * 128, 128), 128)
-            h0, h1 = hs[0, :, at], hs[1, :, at]
-            h0 = jnp.concatenate([h0, h0], axis=0)
-            h1 = jnp.concatenate([h1, h1], axis=0)
-            for t in ts:
-                for p in range(4):
-                    here = pl.ds(p * 16, 16)
-                    seed = seed_ref[t, here, :]
-                    u0 = ((rounds(h0 ^ seed) & LOW).astype(F32) + 0.5) * UNIT
-                    r = jnp.sqrt(-2.0 * jnp.log(u0))
-                    a = (rounds(h1 ^ seed) & LOW).astype(F32) + (0.5 - 4194304.0)
-                    y = (jnp.abs(a) - 2097152.0) * (4.0 * UNIT)
-                    e = r * sine(y, 2.0)
-                    x = jnp.broadcast_to(xs[t, p:p + 1, at], (16, 128))
-                    z = x + e
-                    q = e * e
-                    if mask is not None:
-                        z = jnp.where(mask, z, 0.0)
-                        q = jnp.where(mask, q, 0.0)
-                    zs[t, here, at] = z.astype(BF16)
-                    sqs[t, here, :] += q
-
-    def first_layer(ts, k, width):
-        at = pl.ds(pl.multiple_of(k * KC, 128), width)
-        left = jnp.concatenate([zs[t, :, at] for t in ts], axis=0)
-        acc[...] += jnp.dot(left, w1s[at, :], preferred_element_type=F32)
+    def target(s, n):
+        power = 1 + 3 * n + 9 * (n * (n - 1) // 2) + 27 * (n * (n - 1) * (n - 2) // 6)
+        a, b = (sum((TREE[4 * s + i][0][d] % 4) * 4**i for i in range(4)) for d in range(2))
+        return ((my + (b // power) % 4) % 4) * 4 + (mx + (a // power) % 4) % 4
+
+    def noise(t):
+        for p in range(4):
+            here = pl.ds(p * 16, 16)
+            seed = seed_ref[t, here, :]
+            squares = None
+            for l in range(LANES // 128):
+                at = pl.ds(l * 128, 128)
+                h0, h1 = hs[0, :, at], hs[1, :, at]
+                h0 = jnp.concatenate([h0, h0], axis=0)
+                h1 = jnp.concatenate([h1, h1], axis=0)
+                u0 = ((rounds(h0 ^ seed) & LOW).astype(F32) + 0.5) * UNIT
+                w = jnp.maximum(-2.0 * jnp.log(u0), 1e-9)
+                r = w * lax.rsqrt(w)
+                a = (rounds(h1 ^ seed) & LOW).astype(F32) + (0.5 - 4194304.0)
+                y = (jnp.abs(a) - 2097152.0) * (4.0 * UNIT)
+                e = r * sine(y, 2.0)
+                z = jnp.broadcast_to(xs[t, p:p + 1, at], (16, 128)) + e
+                q = e * e
+                if l == LANES // 128 - 1:
+                    z = jnp.where(tail_mask, z, 0.0)
+                    q = jnp.where(tail_mask, q, 0.0)
+                zs[t, here, at] = z.astype(BF16)
+                squares = q if squares is None else squares + q
+            sqs[t, here, :] = squares
+
+    def first_layer(s, n):
+        at = pl.ds(pl.multiple_of(n * 256, 256), 256)
+        left = jnp.concatenate([zs[target(s, i)] for i in range(4)], axis=0)
+        acc[:, at] = jnp.dot(left, w1s[:, at], preferred_element_type=F32)
 
     eye = jnp.where(
         lax.broadcasted_iota(I32, (ROWS, 128), 0) == lax.broadcasted_iota(I32, (ROWS, 128), 1), 1.0, 0.0
@@ -211,26 +216,25 @@
             tile += srecv[child]
         return value.astype(BF16), tile
 
-    loads[0].wait()
-    loads[1].wait()
-
-    for s in range(4):
-        ts = [((my + b + 4) % 4) * 4 + (mx + a + 4) % 4 for (a, b), _ in TREE[4 * s:4 * s + 4]]
-        acc[...] = jnp.zeros_like(acc)
-        noise(ts, 0, KC, None)
-
-        def inner(k, ts=ts):
-            first_layer(ts, k - 1, KC)
-            noise(ts, k, KC, None)
-
-        each(1, 12, inner)
-        first_layer(ts, 11, KC)
-        noise(ts, 12, 128, tail_mask)
-        first_layer(ts, 12, 128)
+    for s in range(5):
+        if s == 1:
+            loads[0].wait()
+            loads[1].wait()
+
+        def both(n, s=s):
+            if s < 4:
+                noise(target(s, n))
+            if s > 0:
+                first_layer(s - 1, n)
+
+        each(0, 4, both)
         if s == 0:
+            continue
+        if s == 1:
             pl.semaphore_wait(barrier, XY - 1 + 5)
+        ts = [target(s - 1, i) for i in range(4)]
         for i, t in enumerate(ts):
-            n = 4 * s + i
+            n = 4 * s - 4 + i
             value, tile = gathered(n, i, t)
             if n < XY - 1:
                 psend[n] = value
@@ -319,7 +323,52 @@
     def core_copy(n):
         return remote(bsend.at[n], brecv.at[n], b_ss.at[n], b_rs.at[n], sibling)
 
-    def chunk(j):
+    def right_copy(n):
+        return remote(lsend.at[n], lrecv.at[n], l_ss.at[n], l_rs.at[n], chip(zlo + 1))
+
+    def left_copy(n):
+        return remote(rsend.at[n], rrecv.at[n], r_ss.at[n], r_rs.at[n], chip(zlo - 1))
+
+    def chip_sum(n):
+        core_copy(n).wait_recv()
+        return own[n] + brecv[n].astype(F32)
+
+    def go_right(t, b):
+        n = t * NSUB + b
+        tmp[...] = chip_sum((3 - t) * NSUB + b)
+
+        @pl.when(zlo > 0)
+        def _():
+            remote(lsend.at[n], lrecv.at[n], l_ss.at[n], l_rs.at[n], chip(zlo - 1)).wait_recv()
+            tmp[...] += lrecv[n].astype(F32)
+
+        lsend[n] = tmp[...].astype(BF16)
+        right_copy(n).start()
+
+    def go_left(t, b):
+        n = t * NSUB + b
+        tmp[...] = chip_sum(n)
+
+        @pl.when(zlo < 3)
+        def _():
+            remote(rsend.at[n], rrecv.at[n], r_ss.at[n], r_rs.at[n], chip(zlo + 1)).wait_recv()
+            tmp[...] += rrecv[n].astype(F32)
+
+        rsend[n] = tmp[...].astype(BF16)
+        left_copy(n).start()
+
+    def onward(n):
+        r, l = n - LAG * upper, n - LAG * (1 - upper)
+
+        @pl.when((r >= 0) & (r < (3 - zlo) * NSUB))
+        def _():
+            go_right(r // NSUB, r % NSUB)
+
+        @pl.when((l >= 0) & (l < zlo * NSUB))
+        def _():
+            go_left(l // NSUB, l % NSUB)
+
+    def chunk(j, after):
         def there(p):
             slot = (me + p) % XY
             gather_copy(j, slot, slot).wait_recv()
@@ -337,57 +386,18 @@
             bsend[n] = part[0:128].astype(BF16)
             core_copy(n).start()
             own[n] = part[128:256]
+            after(b)
 
         each(0, NSUB, sub)
 
-    def right_copy(n):
-        return remote(lsend.at[n], lrecv.at[n], l_ss.at[n], l_rs.at[n], chip(zlo + 1))
-
-    def left_copy(n):
-        return remote(rsend.at[n], rrecv.at[n], r_ss.at[n], r_rs.at[n], chip(zlo - 1))
-
-    def chip_sum(n):
-        core_copy(n).wait_recv()
-        return own[n] + brecv[n].astype(F32)
-
-    def go_right(t, b):
-        n = t * NSUB + b
-        tmp[...] = chip_sum((3 - t) * NSUB + b)
-
-        @pl.when(zlo > 0)
-        def _():
-            remote(lsend.at[n], lrecv.at[n], l_ss.at[n], l_rs.at[n], chip(zlo - 1)).wait_recv()
-            tmp[...] += lrecv[n].astype(F32)
-
-        lsend[n] = tmp[...].astype(BF16)
-        right_copy(n).start()
-
-    def go_left(t, b):
-        n = t * NSUB + b
-        tmp[...] = chip_sum(n)
-
-        @pl.when(zlo < 3)
-        def _():
-            remote(rsend.at[n], rrecv.at[n], r_ss.at[n], r_rs.at[n], chip(zlo + 1)).wait_recv()
-            tmp[...] += rrecv[n].astype(F32)
-
-        rsend[n] = tmp[...].astype(BF16)
-        left_copy(n).start()
-
-    def onward(n):
-        r, l = n - LAG * upper, n - LAG * (1 - upper)
-
-        @pl.when((r >= 0) & (r < (3 - zlo) * NSUB))
-        def _():
-            go_right(r // NSUB, r % NSUB)
-
-        @pl.when((l >= 0) & (l < zlo * NSUB))
-        def _():
-            go_left(l // NSUB, l % NSUB)
-
     def columns(q):
-        chunk(order(q))
-        lo = (1 - inside) * q * NSUB
+        def after(b):
+            @pl.when((inside == 0) & (q < 3) & (b >= 2))
+            def _():
+                onward(q * NSUB + b - 2)
+
+        chunk(order(q), after)
+        lo = (1 - inside) * (q * NSUB + NSUB - 2)
         hi = (1 - inside) * (q * NSUB + NSUB) + inside * (q // 2) * (1 - q % 2) * (2 * NSUB + LAG)
 
         @pl.when(q < 3)

time: 152 us -> 145 us (0.954)
  Pallas kernels: 141 us -> 133 us
    pallas_call x1, Pallas kernels: 141 us -> 133 us  [shards(): pl.pallas_call(kernel, name='pinn_step', out_shape=(jax.ShapeDtypeStruct(...]
where the time goes in v3:
time: 145 us; the launch traced here: 144 us
  Pallas kernels  133 us (92%)
  local copies, waits for them, and re-layouts  10.4 us (7%)
    pallas_call x1, Pallas kernels, shards(): pl.pallas_call(kernel, name='pinn_step', out_shape=(jax.ShapeDtypeStruct(...  133 us
    unnamed x2, local copies, waits for them, and re-layouts  3.73 us

profile of v3, /device:TPU:1, one launch (start us, length us, event | category | flops | bytes accessed | tf_op | source)
XLA Modules:
  0.0 143.9 jit_solution(4034201340276704151)
XLA Ops:
  0.6 0.9 slice.20
  1.5 0.7 pad.9.w1t_ref
  2.3 0.7 reshape.23
  3.0 0.6 pad.8.coef_ref
  3.6 1.3 reshape.25.w3_ref
  4.9 132.8 %pinn_step.1 = (f32[8,128]{1,0:T(8,128)}, bf16[128,3200]{1,0:T(8,128)(2,1)}, f32[32,1024]{1,0:T(8,128)}) custom-call(s32[16,64]{1,0:T(8,128)} %bitcast.14, s32[1,64]{1,0:T(1,128)} %bitcast.16, f32[1,3200]{1,0:T(1,128)} %pad.8.coef_ref, bf16[3125,1024]{1,0:T(8,128)(2,1)} %bitcast.12, bf16[128,1024]{1,0:T(8,128)(2,1)} %pad.9.w1t_ref, f32[1,1024]{1,0:T(1,128)} %bitcast.15, ...), custom_call_target="tpu_custom_call" | custom-call | tf_op jit(solution)/shard_map/pinn_step/pallas_call | solution.py:501
  137.7 1.3 slice_bitcast_fusion
  139.0 1.2 slice_bitcast_fusion.2
  140.2 2.2 %copy.12 = bf16[128,3125]{0,1:T(8,128)(2,1)} copy(bf16[128,3125]{1,0:T(8,128)(2,1)} %bitcast.13) | data formatting | bytes 1600000
  142.3 1.6 %copy.14 = f32[32,1024]{1,0:T(8,128)} copy(f32[32,1024]{1,0:T(8,128)} %get-tuple-element.25) | data formatting | bytes 262144

commit v4 on v3

--- a/solution.py
+++ b/solution.py
@@ -32,6 +32,13 @@
     ((1, 1), (1, 0)), ((-1, 1), (0, 1)), ((1, -1), (0, -1)), ((0, -1), (0, -1)),
     ((1, 0), (1, 0)), ((-1, 0), (-1, 0)), ((0, 1), (0, 1)), ((0, 0), None),
 )
+
+
+NEAR = ((1, 1), (-1, -1), (1, 0), (0, 1), (-1, 1), (1, -1), (-1, 0), (0, -1))
+RELAY = (((1, 1), (1, 1)), ((1, 1), (0, 1)), ((1, 0), (1, 0)), ((0, 1), (0, 1)), ((-1, -1), (-1, 0)), ((-1, -1), (0, -1)), ((-1, 1), (-1, 0)))
+PASSED = tuple(dict.fromkeys(o for o, _ in RELAY))
+FAR = tuple(((o[0] + m[0] + 1) % 4 - 1, (o[1] + m[1] + 1) % 4 - 1) for o, m in RELAY)
+assert len(set(NEAR + FAR)) == XY - 1 and (0, 0) not in NEAR + FAR
 
 
 def lands(n):
@@ -286,8 +293,30 @@
         h2s[j] = two[:, 256 * j:256 * j + 256]
         d2s[j] = dpre2[:, 256 * j:256 * j + 256]
 
-    def gather_copy(j, t, slot):
-        return remote(dbuf.at[j], dall.at[j, slot], a_ss.at[j * XY + t], a_rs.at[j * XY + slot], plane(t))
+    def at_offset(o):
+        return ((my + o[1] + 4) % 4) * 4 + (mx + o[0] + 4) % 4
+
+    def origin(o):
+        return ((my - o[1] + 4) % 4) * 4 + (mx - o[0] + 4) % 4
+
+    def near_copy(j, k):
+        return remote(dbuf.at[j], dall.at[j, me], a_ss.at[j * XY + k], a_rs.at[j * XY + me], plane(at_offset(NEAR[k])))
+
+    def relay_copy(j, k):
+        slot = origin(RELAY[k][0])
+        return remote(
+            dall.at[j, slot], dall.at[j, slot], a_ss.at[j * XY + 8 + k], a_rs.at[j * XY + slot], toward(RELAY[k][1]))
+
+    def came(j, o):
+        slot = origin(o)
+        remote(dbuf.at[j], dall.at[j, slot], a_ss.at[j * XY], a_rs.at[j * XY + slot], plane(slot)).wait_recv()
+
+    def pass_on(j):
+        for o in PASSED:
+            came(j, o)
+            for k, (first, _) in enumerate(RELAY):
+                if first == o:
+                    relay_copy(j, k).start()
 
     inside, upper = zlo * (3 - zlo) // 2, zlo // 2
 
@@ -295,8 +324,11 @@
         base = (1 - inside) * (3 - q) + inside * ((q % 2) * (q // 2) + (1 - q % 2) * (3 - q // 2))
         return upper * 3 + (1 - 2 * upper) * base
 
-    for q in range(4):
-        each(1, XY, lambda p, q=q: gather_copy(order(q), (me + p) % XY, me).start())
+    def sends(q):
+        for k in range(8):
+            near_copy(order(q), k).start()
+
+    each(0, 4, sends)
 
     lane64 = lax.broadcasted_iota(I32, (ROWS, 128), 1)
     high = dval.astype(BF16)
@@ -318,7 +350,6 @@
         mine = gbuf.at[t // 4, pl.ds(pl.multiple_of((t % 4) * 32, 32), 32)]
         return remote(mine, grecv.at[slot], g_ss.at[t], g_rs.at[slot], plane(t))
 
-    each(1, XY, lambda p: small_copy((me + p) % XY, me).start())
 
     def core_copy(n):
         return remote(bsend.at[n], brecv.at[n], b_ss.at[n], b_rs.at[n], sibling)
@@ -369,11 +400,9 @@
             go_left(l // NSUB, l % NSUB)
 
     def chunk(j, after):
-        def there(p):
-            slot = (me + p) % XY
-            gather_copy(j, slot, slot).wait_recv()
-
-        each(1, XY, there)
+        for o in NEAR + FAR:
+            if o not in PASSED:
+                came(j, o)
         for n, c in enumerate((1 - core, core)):
             block = dall[j, :, :, pl.ds(pl.multiple_of(c * 128, 128), 128)].reshape(XY * ROWS, 128)
             dt[128 * n:128 * n + 128, :] = jnp.transpose(block)
@@ -396,6 +425,14 @@
             def _():
                 onward(q * NSUB + b - 2)
 
+        @pl.when(q < 3)
+        def _():
+            pass_on(order(q + 1))
+
+        @pl.when(q == 2)
+        def _():
+            each(1, XY, lambda p: small_copy((me + p) % XY, me).start())
+
         chunk(order(q), after)
         lo = (1 - inside) * (q * NSUB + NSUB - 2)
         hi = (1 - inside) * (q * NSUB + NSUB) + inside * (q // 2) * (1 - q % 2) * (2 * NSUB + LAG)
@@ -404,6 +441,7 @@
         def _():
             each(lo, hi, onward)
 
+    pass_on(order(0))
     each(0, 4, columns)
 
     def small_there(p):
@@ -471,10 +509,16 @@
     def left_plane(p):
         t = (me + p) % XY
         small_copy(t, me).wait_send()
-        for j in range(4):
-            gather_copy(j, t, me).wait_send()
 
     each(1, XY, left_plane)
+
+    def gather_left(j):
+        for k in range(8):
+            near_copy(j, k).wait_send()
+        for k in range(7):
+            relay_copy(j, k).wait_send()
+
+    each(0, 4, gather_left)
     for n in range(XY - 1):
         partial_copy(n).wait_send()
         stat_copy(n).wait_send()

time: 145 us -> 144 us (level)
  no operation moved by 1% of the time
where the time goes in v4:
time: 144 us
  Pallas kernels  133 us (92%)
  local copies, waits for them, and re-layouts  10.4 us (7%)
    pallas_call x1, Pallas kernels, shards(): pl.pallas_call(kernel, name='pinn_step', out_shape=(jax.ShapeDtypeStruct(...  133 us
    unnamed x2, local copies, waits for them, and re-layouts  3.73 us

profile of v4, /device:TPU:1, one launch (start us, length us, event | category | flops | bytes accessed | tf_op | source)
XLA Modules:
  0.0 143.6 jit_solution(2210800931937625711)
XLA Ops:
  0.6 0.9 slice.20
  1.5 0.7 pad.9.w1t_ref
  2.3 0.7 reshape.23
  3.0 0.6 pad.8.coef_ref
  3.6 1.3 reshape.25.w3_ref
  4.9 132.5 %pinn_step.1 = (f32[8,128]{1,0:T(8,128)}, bf16[128,3200]{1,0:T(8,128)(2,1)}, f32[32,1024]{1,0:T(8,128)}) custom-call(s32[16,64]{1,0:T(8,128)} %bitcast.14, s32[1,64]{1,0:T(1,128)} %bitcast.16, f32[1,3200]{1,0:T(1,128)} %pad.8.coef_ref, bf16[3125,1024]{1,0:T(8,128)(2,1)} %bitcast.12, bf16[128,1024]{1,0:T(8,128)(2,1)} %pad.9.w1t_ref, f32[1,1024]{1,0:T(1,128)} %bitcast.15, ...), custom_call_target="tpu_custom_call" | custom-call | tf_op jit(solution)/shard_map/pinn_step/pallas_call | solution.py:545
  137.4 1.3 slice_bitcast_fusion
  138.7 1.2 slice_bitcast_fusion.2
  139.9 2.2 %copy.12 = bf16[128,3125]{0,1:T(8,128)(2,1)} copy(bf16[128,3125]{1,0:T(8,128)(2,1)} %bitcast.13) | data formatting | bytes 1600000
  142.0 1.6 %copy.14 = f32[32,1024]{1,0:T(8,128)} copy(f32[32,1024]{1,0:T(8,128)} %get-tuple-element.25) | data formatting | bytes 262144

commit v5 on v4

--- a/solution.py
+++ b/solution.py
@@ -72,7 +72,7 @@
 def kernel(
     pert_ref, point_ref, coef_ref, w1_ref, w1t_ref, b1_ref, w2_ref, w3_ref,
     res_ref, grad_ref, g2_ref,
-    seed_ref, pseed_ref, w1s, w2s, zs, xs, hs, sqs, srcs, acc,
+    seed_ref, pseed_ref, coefs, w1s, w2s, zs, xs, hs, sqs, srcs, acc,
     psend, precv, ssend, srecv, zsend, zrecv, tsend, trecv,
     h1s, h2s, d2s, dbuf, dall, dt, own, bsend, brecv, tmp, lsend, lrecv, rsend, rrecv,
     gbuf, grecv, gtot, hsend, hrecv, csend, crecv, fsend, frecv,
@@ -105,11 +105,13 @@
 
     loads = [
         pltpu.make_async_copy(w1_ref.at[pl.ds(0, 3072)], w1s.at[pl.ds(0, 3072)], load_sem.at[0]),
-        pltpu.make_async_copy(w1t_ref, w1s.at[pl.ds(3072, 128)], load_sem.at[1]),
+        pltpu.make_async_copy(w1_ref.at[pl.ds(3072, 48)], w1s.at[pl.ds(3072, 48)], load_sem.at[1]),
         pltpu.make_async_copy(w2_ref, w2s, load_sem.at[2]),
     ]
     for c in loads:
         c.start()
+    w1s[3120:LANES, :] = jnp.zeros((LANES - 3120, HID), BF16)
+    w1s[3120:WIDTH, :] = w1t_ref[...]
     barrier = pltpu.get_barrier_semaphore()
 
     def greet(device):
@@ -132,6 +134,8 @@
     pseed_ref[...] = shuffle_bits(jnp.broadcast_to(spread, (64, 128)))
 
     srcs[...] = jnp.zeros_like(srcs)
+    coefs[...] = jnp.zeros_like(coefs)
+    coefs[:, 0:WIDTH] = coef_ref[...]
     lane8 = lax.broadcasted_iota(I32, (8, 128), 1)
     row8 = lax.broadcasted_iota(I32, (8, 128), 0)
 
@@ -143,7 +147,7 @@
             if n < 2:
                 hs[n, :, at] = shuffle_bits(h)
         h = shuffle_bits(h)
-        coef = jnp.broadcast_to(coef_ref[:, at], (8, 128))
+        coef = jnp.broadcast_to(coefs[:, at], (8, 128))
         for g in range(8):
             v = rounds(h ^ pseed_ref[8 * g:8 * g + 8, :])
             t = (v & LOW).astype(F32) + (0.5 - 4194304.0)
@@ -534,9 +538,9 @@
 
 
 def shards(point_seed, pert_seed, source_coef, w1, b1, w2, w3):
-    coef = jnp.pad(source_coef.reshape(1, WIDTH), ((0, 0), (0, LANES - WIDTH)))
+    coef = source_coef.reshape(1, WIDTH)
     w1t = w1.T
-    tail = jnp.pad(w1t[3072:], ((0, LANES - WIDTH), (0, 0)))
+    tail = w1t[3120:]
     vmem = pl.BlockSpec(memory_space=pltpu.VMEM)
     anyw = pl.BlockSpec(memory_space=pl.ANY)
     dma = lambda n: pltpu.SemaphoreType.DMA((n,))
@@ -550,10 +554,10 @@
             jax.ShapeDtypeStruct((128, LANES), BF16),
             jax.ShapeDtypeStruct((32, HID), F32),
         ),
-        in_specs=[vmem, vmem, vmem, anyw, anyw, vmem, anyw, vmem],
+        in_specs=[vmem, vmem, vmem, anyw, vmem, vmem, anyw, vmem],
         out_specs=(vmem, vmem, vmem),
         scratch_shapes=[
-            v((XY, ROWS, 128), I32), v((64, 128), I32), v((LANES, HID), BF16), v((HID, HID), BF16), v((XY, ROWS, LANES), BF16),
+            v((XY, ROWS, 128), I32), v((64, 128), I32), v((1, LANES), F32), v((LANES, HID), BF16), v((HID, HID), BF16), v((XY, ROWS, LANES), BF16),
             v((XY, 8, LANES), F32), v((2, 8, LANES), I32), v((XY, ROWS, 128), F32), v((XY, 8, 128), F32),
             v((256, HID), F32),
             v((XY, ROWS, HID), BF16), v((XY, ROWS, HID), BF16), v((XY, 8, 128), F32), v((XY, 8, 128), F32),

time: 144 us -> 144 us (level)
  no operation moved by 1% of the time
where the time goes in v5:
time: 144 us
  Pallas kernels  133 us (92%)
  local copies, waits for them, and re-layouts  10.1 us (7%)
    pallas_call x1, Pallas kernels, shards(): pl.pallas_call(kernel, name='pinn_step', out_shape=(jax.ShapeDtypeStruct(...  133 us
    unnamed x2, local copies, waits for them, and re-layouts  3.73 us

profile of v5, /device:TPU:1, one launch (start us, length us, event | category | flops | bytes accessed | tf_op | source)
XLA Modules:
  0.0 143.6 jit_solution(1673900906622631042)
XLA Ops:
  0.6 1.3 slice.20.w1t_ref
  2.0 1.3 reshape.23.coef_ref
  3.3 1.3 reshape.25.w3_ref
  4.6 132.8 %pinn_step.1 = (f32[8,128]{1,0:T(8,128)}, bf16[128,3200]{1,0:T(8,128)(2,1)}, f32[32,1024]{1,0:T(8,128)}) custom-call(s32[16,64]{1,0:T(8,128)} %bitcast.14, s32[1,64]{1,0:T(1,128)} %bitcast.16, f32[1,3125]{1,0:T(1,128)} %reshape.23.coef_ref, bf16[3125,1024]{1,0:T(8,128)(2,1)} %bitcast.12, bf16[5,1024]{1,0:T(8,128)(2,1)} %slice.20.w1t_ref, ...), custom_call_target="tpu_custom_call" | custom-call | tf_op jit(solution)/shard_map/pinn_step/pallas_call | solution.py:549
  137.4 1.3 slice_bitcast_fusion
  138.7 1.2 slice_bitcast_fusion.2
  139.8 2.2 %copy.12 = bf16[128,3125]{0,1:T(8,128)(2,1)} copy(bf16[128,3125]{1,0:T(8,128)(2,1)} %bitcast.13) | data formatting | bytes 1600000
  142.0 1.6 %copy.14 = f32[32,1024]{1,0:T(8,128)} copy(f32[32,1024]{1,0:T(8,128)} %get-tuple-element.25) | data formatting | bytes 262144
